TPU v7x, 128 devices: a whole 4x4x4 slice. The times are simulated.
128 devices in a mesh: seq: 16 (over z, x), inner: 8 (over y, core).
Axes of the slice: x: 4, y: 4, z: 4, core: 2. Of those that a mesh axis runs over, the one named last changes fastest.
Arguments:
- log_mel: bfloat16 [114688, 320], P(('seq', 'inner')), may hold values from -6 to 6
- lengths: int32 [128, 4], replicated, may hold values from 1 to 893, as said below
- first_kernel: bfloat16 [9, 128], replicated, may hold values from -2 to 2
- first_bias: float32 [128], replicated, may hold values from -3 to 3
- second_kernel: bfloat16 [1152, 128], replicated, may hold values from -0.1875 to 0.1875
- second_bias: float32 [128], replicated, may hold values from -3 to 3
- embed_weight: bfloat16 [2560, 1024], replicated, may hold values from -0.125 to 0.125
- norm_gain: float32 [1024], replicated, may hold values from 0.1 to 1.9
- head_weight: bfloat16 [1024, 3072], replicated
- output_weight: bfloat16 [1024, 1024], replicated, may hold values from -0.1875 to 0.1875
Outputs:
- encoded: bfloat16 [65536, 1024], P(('seq', 'inner'))
Inputs may be any that keep to these rules, and one draw needn't show every extreme that they name: `lengths`: every length is 1 or more. The frames of owner d begin at d * 512 + e_d with e_d between -192 and 192; e_0 = 0, the frames of all owners together are exactly 65536, and in every draw some owner has e_d = 192 and another e_d = -192. In every draw some utterance has exactly 893 frames.
All inputs are finite; a program needn't handle non-finite values.
Results may differ from a plain program's by a relative error of at most 0.008.
The roundings to bfloat16 on the way count: a program that leaves them out, or rounds other values in their place, can miss the bound.
Values may be sent and summed in bfloat16 or wider, within the bound.
A program may use at most 256 MiB of HBM per device.

v0:
```python
import functools

import jax
import jax.numpy as jnp
from jax import lax
from jax.experimental import pallas as pl
from jax.experimental.pallas import tpu as pltpu
from jax.sharding import PartitionSpec as P

HEADS = 16
SPAN = 64
LEFT_SPANS = 4
CTX = 320
SHARD = 512
MARGIN = 192
MEL = 80
CH = 128
D = 1024
BINS = 20
PAD = 16
LOW_ROWS = MARGIN + PAD
AXES = ("seq", "inner")
F32 = jnp.float32
BF16 = jnp.bfloat16


def bounds(device, devices, lens_ref, lens_smem):
    rows = lax.broadcasted_iota(jnp.int32, lens_ref.shape, 0)
    before = jnp.where(rows < device - 1, lens_ref[...].astype(F32), 0.0)
    base = jnp.sum(jnp.sum(before, axis=0, keepdims=True), axis=1, keepdims=True).astype(jnp.int32)
    starts = []
    total = jnp.int32(0)
    for step in (-1, 0, 1):
        owner = device + step
        real = (owner >= 0) & (owner < devices)
        safe = jnp.clip(owner, 0, devices - 1)
        for column in range(lens_smem.shape[1]):
            starts.append(total)
            total = total + jnp.where(real, lens_smem[safe, column], 0)
    return base, starts


def locate(spots, base, starts):
    rel = spots - base
    seg = jnp.zeros_like(rel)
    begin = jnp.zeros_like(rel)
    for start in starts[1:]:
        reached = rel >= start
        seg = seg + reached.astype(jnp.int32)
        begin = jnp.where(reached, start, begin)
    return seg, rel - begin


def codes(seg, pos):
    return seg * 64 + lax.shift_right_arithmetic(pos, 6)


def build_taps(first_kernel, first_bias, kext):
    kext[...] = jnp.zeros_like(kext)
    taps = first_kernel[...].astype(F32)
    for a in range(3):
        for b in range(3):
            row = taps[3 * a + b : 3 * a + b + 1, :]
            kext[5 * a + b : 5 * a + b + 1, 0:CH] = row
            kext[5 * a + b + 2 : 5 * a + b + 3, CH : 2 * CH] = row
    rest = first_bias[...]
    for part in range(3):
        piece = rest.astype(BF16).astype(F32)
        rest = rest - piece
        kext[15 + part : 16 + part, 0:CH] = piece
        kext[15 + part : 16 + part, CH : 2 * CH] = piece


def build_first(kext, w1):
    row = lax.broadcasted_iota(jnp.int32, (256, 32), 0)
    col = lax.broadcasted_iota(jnp.int32, (256, 32), 1)
    tap = (row >= MEL).astype(jnp.int32) + (row >= 2 * MEL).astype(jnp.int32)
    mel = row - MEL * tap
    wide = kext[...].astype(BF16)

    def body(f, carry):
        off = mel - 4 * f + 1
        inside = (off >= 0) & (off <= 4) & (row < 3 * MEL)
        want = jnp.where(inside, 5 * tap + off, jnp.where(row >= 3 * MEL, row - 3 * MEL + 15, -1))
        select = jnp.where(col == want, 1.0, 0.0).astype(BF16)
        block = jnp.dot(select, wide, preferred_element_type=F32)
        w1[:, pl.ds(pl.multiple_of(f * 256, 256), 256)] = block.astype(BF16)
        return carry

    lax.fori_loop(0, BINS, body, 0, unroll=2)


def build_second(second_kernel, w2):
    for a in range(3):
        base = 3 * a * CH
        w2[256 * a : 256 * a + 256, 0:CH] = second_kernel[base + CH : base + 3 * CH, :]
        w2[256 * a : 256 * a + CH, CH : 2 * CH] = jnp.zeros((CH, CH), BF16)
        w2[256 * a + CH : 256 * a + 256, CH : 2 * CH] = second_kernel[base : base + CH, :]


def build_inputs(device, base, starts, raw, low, high, rows32, x):
    count = SHARD + PAD
    spots = device * SHARD - PAD + lax.broadcasted_iota(jnp.int32, (count, 1), 0)
    seg, pos = locate(spots, base, starts)
    owner = lax.shift_right_arithmetic(seg, 2)
    first = MARGIN - PAD
    rows32[0:LOW_ROWS, :] = jnp.where(
        owner[0:LOW_ROWS] == 0, low[...].astype(F32), raw[first : first + LOW_ROWS, :].astype(F32)
    )
    rows32[LOW_ROWS : count - MARGIN, :] = raw[first + LOW_ROWS : first + count - MARGIN, :].astype(F32)
    rows32[count - MARGIN : count, :] = jnp.where(
        owner[count - MARGIN :] == 2,
        high[...].astype(F32),
        raw[first + count - MARGIN : first + count, :].astype(F32),
    )
    joined = pos[PAD:] > 0
    now = rows32[PAD:count, :]
    before = jnp.where(joined, rows32[PAD - 1 : count - 1, :], 0.0)
    ones = jnp.ones((SHARD, 16), F32)
    kept = jnp.where(joined, ones, 0.0)
    x[0:SHARD, :] = jnp.concatenate([before[:, MEL:], kept], axis=1).astype(BF16)
    x[SHARD : 2 * SHARD, :] = jnp.concatenate(
        [before[:, 3 * MEL :], now[:, : 2 * MEL], ones], axis=1
    ).astype(BF16)
    x[2 * SHARD :, :] = jnp.concatenate([now[:, MEL:], ones], axis=1).astype(BF16)


def convolve(x, w1, w2, second_bias, ycat, lower, second_out):
    lower[...] = jnp.zeros_like(lower)
    bias = second_bias[...]

    def body(f, carry):
        block = w1[:, pl.ds(pl.multiple_of(f * 256, 256), 256)]
        for a in range(3):
            y = jnp.dot(x[a * SHARD : (a + 1) * SHARD, :], block, preferred_element_type=F32)
            ycat[:, 256 * a : 256 * a + 256] = jnp.maximum(y, 0.0).astype(BF16)
        r = jnp.dot(ycat[...], w2[...], preferred_element_type=F32)
        out = jnp.maximum(r[:, :CH] + lower[...] + bias, 0.0).astype(BF16)
        lower[...] = r[:, CH:]
        second_out[:, pl.ds(pl.multiple_of(f * CH, CH), CH)] = out
        return carry

    lax.fori_loop(0, BINS, body, 0)


def front_kernel(
    raw,
    low,
    high,
    lens_ref,
    lens_smem,
    first_kernel,
    first_bias,
    second_kernel,
    second_bias,
    gain,
    embed_hbm,
    head_hbm,
    embedded,
    normed,
    packed,
    kext,
    w1,
    w2,
    rows32,
    x,
    ycat,
    lower,
    second_out,
    embed_w,
    head_w,
    sems,
):
    load_embed = pltpu.make_async_copy(embed_hbm, embed_w, sems.at[0])
    load_head = pltpu.make_async_copy(head_hbm, head_w, sems.at[1])
    load_embed.start()
    load_head.start()
    device = lax.axis_index(AXES)
    devices = lax.axis_size(AXES)
    base, starts = bounds(device, devices, lens_ref, lens_smem)
    build_taps(first_kernel, first_bias, kext)
    build_first(kext, w1)
    build_second(second_kernel, w2)
    build_inputs(device, base, starts, raw, low, high, rows32, x)
    convolve(x, w1, w2, second_bias, ycat, lower, second_out)
    load_embed.wait()

    def embed_step(n, carry):
        cols = pl.ds(pl.multiple_of(n * 256, 256), 256)
        embedded[:, cols] = jnp.dot(
            second_out[...], embed_w[:, cols], preferred_element_type=F32
        ).astype(BF16)
        return carry

    lax.fori_loop(0, D // 256, embed_step, 0)

    def norm_step(r, carry):
        rows = pl.ds(pl.multiple_of(r * 64, 64), 64)
        values = embedded[rows, :].astype(F32)
        center = values - jnp.mean(values, axis=1, keepdims=True)
        spread = jnp.mean(center * center, axis=1, keepdims=True)
        normed[rows, :] = (center * lax.rsqrt(spread + 1e-05) * gain[...]).astype(BF16)
        return carry

    lax.fori_loop(0, SHARD // 64, norm_step, 0)
    load_head.wait()

    def head_step(n, carry):
        cols = pl.ds(pl.multiple_of(n * 256, 256), 256)
        packed[:, cols] = jnp.dot(
            normed[...], head_w[:, cols], preferred_element_type=F32
        ).astype(BF16)
        return carry

    lax.fori_loop(0, 3 * D // 256, head_step, 0)


def attend_kernel(
    packed,
    embedded,
    before,
    after,
    lens_ref,
    lens_smem,
    head_hbm,
    out_hbm,
    encoded,
    keys,
    vals,
    mixed,
    hide,
    head_w,
    out_w,
    sems,
):
    load_head = pltpu.make_async_copy(head_hbm.at[:, D:], head_w, sems.at[0])
    load_out = pltpu.make_async_copy(out_hbm, out_w, sems.at[1])
    load_head.start()
    load_out.start()
    device = lax.axis_index(AXES)
    devices = lax.axis_size(AXES)
    base, starts = bounds(device, devices, lens_ref, lens_smem)
    key_rows = CTX + SHARD + SPAN
    keys[CTX : CTX + SHARD, :] = packed[:, D : 2 * D]
    vals[CTX : CTX + SHARD, :] = packed[:, 2 * D :]
    spots = device * SHARD - CTX + lax.broadcasted_iota(jnp.int32, (1, key_rows), 1)
    key_code = codes(*locate(spots, base, starts))
    key_code = jnp.where((spots >= 0) & (spots < devices * SHARD), key_code, -1000)
    for block in range(4):
        q_spots = device * SHARD + block * 128 + lax.broadcasted_iota(jnp.int32, (128, 1), 0)
        q_code = codes(*locate(q_spots, base, starts))
        gap = q_code - key_code[:, block * 128 : block * 128 + 512]
        hide[block] = jnp.where((gap >= 0) & (gap <= LEFT_SPANS), 0.0, -1e30)
    load_head.wait()

    def context_step(n, carry):
        cols = pl.ds(pl.multiple_of(n * 256, 256), 256)
        for src, width in ((0, keys), (D, vals)):
            block = head_w[:, pl.ds(pl.multiple_of(n * 256 + src, 256), 256)]
            width[0:CTX, cols] = jnp.dot(before[...], block, preferred_element_type=F32).astype(BF16)
            width[CTX + SHARD :, cols] = jnp.dot(
                after[...], block, preferred_element_type=F32
            ).astype(BF16)
        return carry

    lax.fori_loop(0, D // 256, context_step, 0)
    left = lax.broadcasted_iota(jnp.int32, (128, CH), 1) < 64
    ones = jnp.ones((512, CH), BF16)

    def head_step(step, carry):
        block = step // 8
        pair = step - block * 8
        cols = pl.ds(pl.multiple_of(pair * CH, CH), CH)
        q_rows = pl.ds(pl.multiple_of(block * 128, 128), 128)
        k_rows = pl.ds(pl.multiple_of(block * 128, 128), 512)
        q = packed[q_rows, cols] * BF16(0.125)
        k = keys[k_rows, cols]
        v = jnp.concatenate([vals[k_rows, cols], ones], axis=1)
        outs = []
        for half in (left, jnp.logical_not(left)):
            s = lax.dot_general(
                jnp.where(half, q, BF16(0)),
                k,
                (((1,), (1,)), ((), ())),
                preferred_element_type=F32,
            )
            s = s + hide[block]
            p = jnp.exp(s - jnp.max(s, axis=1, keepdims=True)).astype(BF16)
            o = jnp.dot(p, v, preferred_element_type=F32)
            outs.append(o[:, :CH] / o[:, CH:])
        mixed[q_rows, cols] = jnp.where(left, outs[0], outs[1]).astype(BF16)
        return carry

    lax.fori_loop(0, 32, head_step, 0)
    load_out.wait()

    def out_step(n, carry):
        cols = pl.ds(pl.multiple_of(n * 256, 256), 256)
        total = embedded[:, cols].astype(F32) + jnp.dot(
            mixed[...], out_w[:, cols], preferred_element_type=F32
        )
        encoded[:, cols] = total.astype(BF16)
        return carry

    lax.fori_loop(0, D // 256, out_step, 0)


VMEM = pl.BlockSpec(memory_space=pltpu.VMEM)
SMEM = pl.BlockSpec(memory_space=pltpu.SMEM)
HBM = pl.BlockSpec(memory_space=pl.ANY)


def front(raw, low, high, lengths, first_kernel, first_bias, second_kernel, second_bias, gain, embed_w, head_w):
    return pl.pallas_call(
        front_kernel,
        out_shape=[
            jax.ShapeDtypeStruct((SHARD, D), BF16),
            jax.ShapeDtypeStruct((SHARD, D), BF16),
            jax.ShapeDtypeStruct((SHARD, 3 * D), BF16),
        ],
        in_specs=[VMEM, VMEM, VMEM, VMEM, SMEM, VMEM, VMEM, VMEM, VMEM, VMEM, HBM, HBM],
        out_specs=[VMEM] * 3,
        scratch_shapes=[
            pltpu.VMEM((32, 256), F32),
            pltpu.VMEM((256, BINS * 256), BF16),
            pltpu.VMEM((768, 256), BF16),
            pltpu.VMEM((SHARD + PAD, 4 * MEL), F32),
            pltpu.VMEM((3 * SHARD, 256), BF16),
            pltpu.VMEM((SHARD, 768), BF16),
            pltpu.VMEM((SHARD, CH), F32),
            pltpu.VMEM((SHARD, BINS * CH), BF16),
            pltpu.VMEM(embed_w.shape, BF16),
            pltpu.VMEM(head_w.shape, BF16),
            pltpu.SemaphoreType.DMA((2,)),
        ],
        compiler_params=pltpu.CompilerParams(vmem_limit_bytes=56 * 2**20),
        name="front",
    )(raw, low, high, lengths, lengths, first_kernel, first_bias, second_kernel, second_bias, gain, embed_w, head_w)


def attention(packed, embedded, before, after, lengths, head_w, out_w):
    key_rows = CTX + SHARD + SPAN
    return pl.pallas_call(
        attend_kernel,
        out_shape=jax.ShapeDtypeStruct((SHARD, D), BF16),
        in_specs=[VMEM, VMEM, VMEM, VMEM, VMEM, SMEM, HBM, HBM],
        out_specs=VMEM,
        scratch_shapes=[
            pltpu.VMEM((key_rows, D), BF16),
            pltpu.VMEM((key_rows, D), BF16),
            pltpu.VMEM((SHARD, D), BF16),
            pltpu.VMEM((4, 128, 512), F32),
            pltpu.VMEM((D, 2 * D), BF16),
            pltpu.VMEM((D, D), BF16),
            pltpu.SemaphoreType.DMA((2,)),
        ],
        compiler_params=pltpu.CompilerParams(vmem_limit_bytes=56 * 2**20),
        name="attend",
    )(packed, embedded, before, after, lengths, lengths, head_w, out_w)


def shifted(value, by):
    size = lax.axis_size(AXES)
    pairs = [(i, i + by) for i in range(size) if 0 <= i + by < size]
    return lax.ppermute(value, AXES, pairs)


def on_device(
    log_mel,
    lengths,
    first_kernel,
    first_bias,
    second_kernel,
    second_bias,
    embed_weight,
    norm_gain,
    head_weight,
    output_weight,
):
    cap = log_mel.shape[0]
    low = shifted(log_mel[cap - LOW_ROWS :], 1)
    high = shifted(log_mel[:MARGIN], -1)
    embedded, normed, packed = front(
        log_mel,
        low,
        high,
        lengths,
        first_kernel,
        first_bias.reshape(1, -1),
        second_kernel,
        second_bias.reshape(1, -1),
        norm_gain.reshape(1, -1),
        embed_weight,
        head_weight,
    )
    before = shifted(normed[SHARD - CTX :], 1)
    after = shifted(normed[:SPAN], -1)
    return attention(packed, embedded, before, after, lengths, head_weight, output_weight)


def solution(mesh):
    return jax.shard_map(
        on_device,
        mesh=mesh,
        in_specs=(P(AXES, None), P(), P(), P(), P(), P(), P(), P(), P(), P()),
        out_specs=P(AXES, None),
        check_vma=False,
    )
```

profile of v0, /device:TPU:96, one launch (start us, length us, event | category | flops | bytes accessed | tf_op | source)
XLA Modules:
  0.0 92.1 jit_solution(7798003408425924187)
XLA Ops:
  0.0 1.4 %copy.13.raw = bf16[896,320]{1,0:T(8,128)(2,1)S(1)} copy(bf16[896,320]{0,1:T(8,128)(2,1)} %param.10) | data formatting | bytes 1146880 | tf_op args[0]
  1.4 0.0 copy-start
  1.4 1.9 %collective-permute-start = (bf16[208,320]{1,0:T(8,128)(2,1)S(1)}, bf16[208,320]{1,0:T(8,128)(2,1)S(1)}, u32[]{:S(2)}, u32[]{:S(2)}) collective-permute-start(bf16[208,320]{1,0:T(8,128)(2,1)S(1)} %slice.16), channel_id=1, source_target_pairs={{0,1},{1,2},{2,3},{3,4},{4,5},{5,6},{6,7},{7,8},{8,9},{9,10},{10,1... | collective-permute-start | bytes 399368 | tf_op jit(solution)/shard_map/ppermute | solution.py:365
  3.4 7.9 %collective-permute-start.1 = (bf16[192,320]{1,0:T(8,128)(2,1)S(1)}, bf16[192,320]{1,0:T(8,128)(2,1)S(1)}, u32[]{:S(2)}, u32[]{:S(2)}) collective-permute-start(bf16[192,320]{1,0:T(8,128)(2,1)S(1)} %slice.17), channel_id=1, source_target_pairs={{1,0},{2,1},{3,2},{4,3},{5,4},{6,5},{7,6},{8,7},{9,8},{10,9},{11,1... | collective-permute-start | bytes 368648 | tf_op jit(solution)/shard_map/ppermute | solution.py:365
  11.3 1.4 %copy.14.lens_ref.lens_smem = s32[128,4]{1,0:T(8,128)} copy(s32[128,4]{0,1:T(4,128)} %param.11) | data formatting | bytes 4096 | tf_op args[1]
  12.7 1.2 %collective-permute-done.1.high = bf16[192,320]{1,0:T(8,128)(2,1)S(1)} collective-permute-done((bf16[192,320]{1,0:T(8,128)(2,1)S(1)}, bf16[192,320]{1,0:T(8,128)(2,1)S(1)}, u32[]{:S(2)}, u32[]{:S(2)}) %collective-permute-start.1) | collective-permute-done | bytes 122912 | tf_op jit(solution)/shard_map/ppermute | solution.py:365
  13.9 0.0 copy-start.3
  13.9 0.0 collective-permute-done.low
  13.9 0.0 copy-start.2
  13.9 0.0 copy-done
  13.9 0.7 copy-done.3
  14.6 0.0 copy-done.2
  14.6 31.6 %front.1 = (bf16[512,1024]{1,0:T(8,128)(2,1)}, bf16[512,1024]{1,0:T(8,128)(2,1)}, bf16[512,3072]{1,0:T(8,128)(2,1)}) custom-call(bf16[896,320]{1,0:T(8,128)(2,1)} %copy-done, bf16[208,320]{1,0:T(8,128)(2,1)} %copy-done.2, bf16[192,320]{1,0:T(8,128)(2,1)} %copy-done.3, s32[128,4]{1,0:T(8,128)} %copy.14.lens_ref.lens_smem, s32[128,4]{1,0:T(8,128)} %copy.14.lens_ref.lens_smem, ...), custom_call_target="tpu_custom_call" | custom-call | tf_op jit(solution)/shard_map/front/pallas_call | solution.py:314
  46.3 1.1 %slice.14 = bf16[320,1024]{1,0:T(8,128)(2,1)S(1)} slice(bf16[512,1024]{1,0:T(8,128)(2,1)} %get-tuple-element.10), slice={[192:512], [0:1024]} | slice | bytes 1310720 | tf_op jit(solution)/shard_map/slice | solution.py:396
  47.4 1.9 %collective-permute-start.2 = (bf16[320,1024]{1,0:T(8,128)(2,1)S(1)}, bf16[320,1024]{1,0:T(8,128)(2,1)S(1)}, u32[]{:S(2)}, u32[]{:S(2)}) collective-permute-start(bf16[320,1024]{1,0:T(8,128)(2,1)S(1)} %slice.14), channel_id=1, source_target_pairs={{0,1},{1,2},{2,3},{3,4},{4,5},{5,6},{6,7},{7,8},{8,9},{9,10},{10,1... | collective-permute-start | bytes 1966088 | tf_op jit(solution)/shard_map/ppermute | solution.py:365
  49.3 0.9 slice.15
  50.3 8.0 %collective-permute-start.3 = (bf16[64,1024]{1,0:T(8,128)(2,1)S(1)}, bf16[64,1024]{1,0:T(8,128)(2,1)S(1)}, u32[]{:S(2)}, u32[]{:S(2)}) collective-permute-start(bf16[64,1024]{1,0:T(8,128)(2,1)S(1)} %slice.15), channel_id=1, source_target_pairs={{1,0},{2,1},{3,2},{4,3},{5,4},{6,5},{7,6},{8,7},{9,8},{10,9},{11,1... | collective-permute-start | bytes 393224 | tf_op jit(solution)/shard_map/ppermute | solution.py:365
  58.3 2.5 %collective-permute-done.3.after = bf16[64,1024]{1,0:T(8,128)(2,1)S(1)} collective-permute-done((bf16[64,1024]{1,0:T(8,128)(2,1)S(1)}, bf16[64,1024]{1,0:T(8,128)(2,1)S(1)}, u32[]{:S(2)}, u32[]{:S(2)}) %collective-permute-start.3) | collective-permute-done | bytes 131104 | tf_op jit(solution)/shard_map/ppermute | solution.py:365
  60.8 0.0 copy-start.4
  60.8 2.9 %collective-permute-done.2.before = bf16[320,1024]{1,0:T(8,128)(2,1)S(1)} collective-permute-done((bf16[320,1024]{1,0:T(8,128)(2,1)S(1)}, bf16[320,1024]{1,0:T(8,128)(2,1)S(1)}, u32[]{:S(2)}, u32[]{:S(2)}) %collective-permute-start.2) | collective-permute-done | bytes 655392 | tf_op jit(solution)/shard_map/ppermute | solution.py:365
  63.7 0.0 copy-start.1
  63.7 0.0 copy-done.4
  63.7 0.8 copy-done.1
  64.5 27.6 %attend.1 = bf16[512,1024]{1,0:T(8,128)(2,1)} custom-call(bf16[512,3072]{1,0:T(8,128)(2,1)} %get-tuple-element.8.packed, bf16[512,1024]{1,0:T(8,128)(2,1)} %get-tuple-element.9.embedded, bf16[320,1024]{1,0:T(8,128)(2,1)} %copy-done.1, bf16[64,1024]{1,0:T(8,128)(2,1)} %copy-done.4, s32[128,4]{1,0:T(8,128)} %copy.14.lens_ref.lens_smem, ...), custom_call_target="tpu_custom_call" | custom-call | tf_op jit(solution)/shard_map/attend/pallas_call | solution.py:343
  (2 shorter events, 0.0 us)
Async XLA Ops:
  1.4 12.5 %copy-start = (bf16[896,320]{1,0:T(8,128)(2,1)}, bf16[896,320]{1,0:T(8,128)(2,1)S(1)}, u32[]{:S(2)}) copy-start(bf16[896,320]{1,0:T(8,128)(2,1)S(1)} %copy.13.raw) | copy-start | bytes 1720324
  1.4 12.5 %collective-permute-start = (bf16[208,320]{1,0:T(8,128)(2,1)S(1)}, bf16[208,320]{1,0:T(8,128)(2,1)S(1)}, u32[]{:S(2)}, u32[]{:S(2)}) collective-permute-start(bf16[208,320]{1,0:T(8,128)(2,1)S(1)} %slice.16), channel_id=1, source_target_pairs={{0,1},{1,2},{2,3},{3,4},{4,5},{5,6},{6,7},{7,8},{8,9},{9,10},{10,1... | collective-permute-start | bytes 399368 | tf_op jit(solution)/shard_map/ppermute | solution.py:365
  3.4 10.5 %collective-permute-start.1 = (bf16[192,320]{1,0:T(8,128)(2,1)S(1)}, bf16[192,320]{1,0:T(8,128)(2,1)S(1)}, u32[]{:S(2)}, u32[]{:S(2)}) collective-permute-start(bf16[192,320]{1,0:T(8,128)(2,1)S(1)} %slice.17), channel_id=1, source_target_pairs={{1,0},{2,1},{3,2},{4,3},{5,4},{6,5},{7,6},{8,7},{9,8},{10,9},{11,1... | collective-permute-start | bytes 368648 | tf_op jit(solution)/shard_map/ppermute | solution.py:365
  13.9 0.7 copy-start.3
  13.9 0.7 copy-start.2
  47.4 16.3 %collective-permute-start.2 = (bf16[320,1024]{1,0:T(8,128)(2,1)S(1)}, bf16[320,1024]{1,0:T(8,128)(2,1)S(1)}, u32[]{:S(2)}, u32[]{:S(2)}) collective-permute-start(bf16[320,1024]{1,0:T(8,128)(2,1)S(1)} %slice.14), channel_id=1, source_target_pairs={{0,1},{1,2},{2,3},{3,4},{4,5},{5,6},{6,7},{7,8},{8,9},{9,10},{10,1... | collective-permute-start | bytes 1966088 | tf_op jit(solution)/shard_map/ppermute | solution.py:365
  50.3 10.5 %collective-permute-start.3 = (bf16[64,1024]{1,0:T(8,128)(2,1)S(1)}, bf16[64,1024]{1,0:T(8,128)(2,1)S(1)}, u32[]{:S(2)}, u32[]{:S(2)}) collective-permute-start(bf16[64,1024]{1,0:T(8,128)(2,1)S(1)} %slice.15), channel_id=1, source_target_pairs={{1,0},{2,1},{3,2},{4,3},{5,4},{6,5},{7,6},{8,7},{9,8},{10,9},{11,1... | collective-permute-start | bytes 393224 | tf_op jit(solution)/shard_map/ppermute | solution.py:365
  60.8 2.9 %copy-start.4 = (bf16[64,1024]{1,0:T(8,128)(2,1)}, bf16[64,1024]{1,0:T(8,128)(2,1)S(1)}, u32[]{:S(2)}) copy-start(bf16[64,1024]{1,0:T(8,128)(2,1)S(1)} %collective-permute-done.3.after) | copy-start | bytes 393220
  63.7 0.8 copy-start.1
where the time goes:
time: 92.5 us; the launch traced here: 92.1 us
  Pallas kernels  59.2 us (64%)
  starting transfers between devices  19.7 us (21%)
  waiting for transfers between devices  6.65 us (7%)
  local copies, waits for them, and re-layouts  6.46 us (7%)
    pallas_call x1, Pallas kernels, front(): pl.pallas_call(front_kernel, out_shape=[jax.ShapeDtypeStruct((SHARD, D),...  31.6 us
    pallas_call x1, Pallas kernels, attention(): pl.pallas_call(attend_kernel, out_shape=jax.ShapeDtypeStruct((SHARD, D),...  27.6 us
    ppermute x4, starting transfers between devices, shifted(): return lax.ppermute(value, AXES, pairs)  19.7 us
    ppermute x4, waiting for transfers between devices, shifted(): return lax.ppermute(value, AXES, pairs)  6.65 us
    unnamed x12, local copies, waits for them, and re-layouts  4.37 us
  transfers between devices with their start and end apart: 4, of which 3 were waited for; matrix products, arithmetic and copies ran while one was open for 3% of the time, Pallas kernels for 0%

commit v1 on v0

v1 whole, which is shorter than its diff:
```python
import jax
import jax.numpy as jnp
from jax import lax
from jax.experimental import pallas as pl
from jax.experimental.pallas import tpu as pltpu
from jax.sharding import PartitionSpec as P

SPAN = 64
LEFT_SPANS = 4
CTX = 320
SHARD = 512
MARGIN = 192
MEL = 80
CH = 128
D = 1024
BINS = 20
CUT = 192
WIDE = 640
SIDE = 256
QB = 128
QK = 512
KEY_ROWS = CTX + SHARD + SPAN
AXES = ("seq", "inner")
F32 = jnp.float32
BF16 = jnp.bfloat16
MESH = pl.DeviceIdType.MESH


def bounds(device, devices, lens_ref, lens_smem):
    owners = lax.broadcasted_iota(jnp.int32, lens_ref.shape, 1)
    before = jnp.where(owners < device - 1, lens_ref[...].astype(F32), 0.0)
    base = jnp.sum(jnp.sum(before, axis=0, keepdims=True), axis=1, keepdims=True).astype(jnp.int32)
    starts = []
    total = jnp.int32(0)
    for step in (-1, 0, 1):
        owner = device + step
        real = (owner >= 0) & (owner < devices)
        safe = lax.rem(owner + devices, devices)
        for column in range(lens_smem.shape[0]):
            starts.append(total)
            total = total + jnp.where(real, lens_smem[column, safe], 0)
    return base, starts


def locate(spots, base, starts):
    rel = spots - base
    seg = jnp.zeros_like(rel)
    begin = jnp.zeros_like(rel)
    for start in starts[1:]:
        reached = rel >= start
        seg = seg + reached.astype(jnp.int32)
        begin = jnp.where(reached, start, begin)
    return seg, rel - begin


def codes(seg, pos):
    return seg * 64 + lax.shift_right_arithmetic(pos, 6)


def build_taps(first_kernel, first_bias, kext):
    kext[...] = jnp.zeros_like(kext)
    taps = first_kernel[...].astype(F32)
    for a in range(3):
        for b in range(3):
            row = taps[3 * a + b : 3 * a + b + 1, :]
            kext[5 * a + b : 5 * a + b + 1, 0:CH] = row
            kext[5 * a + b + 2 : 5 * a + b + 3, CH : 2 * CH] = row
    rest = first_bias[...]
    for part in range(3):
        piece = rest.astype(BF16).astype(F32)
        rest = rest - piece
        kext[15 + part : 16 + part, 0:CH] = piece
        kext[15 + part : 16 + part, CH : 2 * CH] = piece


def build_first(kext, w1):
    row = lax.broadcasted_iota(jnp.int32, (256, 32), 0)
    col = lax.broadcasted_iota(jnp.int32, (256, 32), 1)
    tap = (row >= MEL).astype(jnp.int32) + (row >= 2 * MEL).astype(jnp.int32)
    mel = row - MEL * tap
    wide = kext[...].astype(BF16)

    def body(f, carry):
        off = mel - 4 * f + 1
        inside = (off >= 0) & (off <= 4) & (row < 3 * MEL)
        want = jnp.where(inside, 5 * tap + off, jnp.where(row >= 3 * MEL, row - 3 * MEL + 15, -1))
        select = jnp.where(col == want, 1.0, 0.0).astype(BF16)
        block = jnp.dot(select, wide, preferred_element_type=F32)
        w1[:, pl.ds(pl.multiple_of(f * 256, 256), 256)] = block.astype(BF16)
        return carry

    lax.fori_loop(0, BINS, body, 0, unroll=4)


def build_second(second_kernel, w2):
    for a in range(3):
        base = 3 * a * CH
        w2[256 * a : 256 * a + 256, 0:CH] = second_kernel[base + CH : base + 3 * CH, :]
        w2[256 * a : 256 * a + CH, CH : 2 * CH] = jnp.zeros((CH, CH), BF16)
        w2[256 * a + CH : 256 * a + 256, CH : 2 * CH] = second_kernel[base : base + CH, :]


def select_rows(device, base, starts, raw, low, high, rows32):
    spots = device * SHARD - 64 + lax.broadcasted_iota(jnp.int32, (1, WIDE), 1)
    seg, unused_pos = locate(spots, base, starts)
    owner = lax.shift_right_arithmetic(seg, 2)
    parts = [
        jnp.where(owner[:, :SIDE] == 0, low[...].astype(F32), raw[:, 128:384].astype(F32)),
        raw[:, 384:512].astype(F32),
        jnp.where(owner[:, WIDE - SIDE :] == 2, high[...].astype(F32), raw[:, 512:768].astype(F32)),
    ]
    rows32[...] = jnp.concatenate(parts, axis=1).T


def build_inputs(begin, count, joined, rows32, x):
    here = joined[begin : begin + count]
    now = rows32[64 + begin : 64 + begin + count, :]
    before = jnp.where(here, rows32[63 + begin : 63 + begin + count, :], 0.0)
    ones = jnp.ones((count, 16), F32)
    kept = jnp.where(here, ones, 0.0)
    x[0:count, :] = jnp.concatenate([before[:, MEL:], kept], axis=1).astype(BF16)
    x[count : 2 * count, :] = jnp.concatenate(
        [before[:, 3 * MEL :], now[:, : 2 * MEL], ones], axis=1
    ).astype(BF16)
    x[2 * count :, :] = jnp.concatenate([now[:, MEL:], ones], axis=1).astype(BF16)


def convolve(count, x, w1, w2, second_bias, ycat, lower, second_out):
    bias = second_bias[...]
    lower[0, 0:count, :] = jnp.zeros((count, CH), F32)

    def body(step, carry):
        for u in range(10):
            slot = u % 2
            f = step * 10 + u
            block = w1[:, pl.ds(pl.multiple_of(f * 256, 256), 256)]
            for a in range(3):
                y = jnp.dot(x[a * count : (a + 1) * count, :], block, preferred_element_type=F32)
                ycat[slot, 0:count, 256 * a : 256 * a + 256] = jnp.maximum(y, 0.0).astype(BF16)
            r = jnp.dot(ycat[slot, 0:count, :], w2[...], preferred_element_type=F32)
            out = jnp.maximum(r[:, :CH] + lower[slot, 0:count, :] + bias, 0.0).astype(BF16)
            lower[1 - slot, 0:count, :] = r[:, CH:]
            second_out[0:count, pl.ds(pl.multiple_of(f * CH, CH), CH)] = out
        return carry

    lax.fori_loop(0, BINS // 10, body, 0)


def embed_rows(begin, count, second_out, embed_w, embedded):
    embedded[begin : begin + count, :] = jnp.dot(
        second_out[0:count, :], embed_w[...], preferred_element_type=F32
    ).astype(BF16)


def norm_rows(begin, count, embedded, gain, normed):
    def step(r, carry):
        rows = pl.ds(pl.multiple_of(begin + r * 64, 64), 64)
        values = embedded[rows, :].astype(F32)
        center = values - jnp.mean(values, axis=1, keepdims=True)
        spread = jnp.mean(center * center, axis=1, keepdims=True)
        normed[rows, :] = (center * lax.rsqrt(spread + 1e-05) * gain[...]).astype(BF16)
        return carry

    lax.fori_loop(0, count // 64, step, 0)


def build_hide(device, devices, base, starts, hide):
    spots = device * SHARD - CTX + lax.broadcasted_iota(jnp.int32, (1, KEY_ROWS), 1)
    key_code = codes(*locate(spots, base, starts))
    key_code = jnp.where((spots >= 0) & (spots < devices * SHARD), key_code, -1000)
    for block in range(SHARD // QB):
        q_spots = device * SHARD + block * QB + lax.broadcasted_iota(jnp.int32, (QB, 1), 0)
        q_code = codes(*locate(q_spots, base, starts))
        gap = q_code - key_code[:, block * QB : block * QB + QK]
        hide[block] = jnp.where((gap >= 0) & (gap <= LEFT_SPANS), 0.0, -1e30)


def attend_block(block, queries, keys, vals, hide, mixed):
    rows = pl.ds(pl.multiple_of(block * QB, QB), QB)
    k_rows = pl.ds(pl.multiple_of(block * QB, QB), QK)
    left = lax.broadcasted_iota(jnp.int32, (QB, CH), 1) < 64
    ones = jnp.ones((QK, CH), BF16)
    for pair in range(D // CH):
        cols = slice(pair * CH, pair * CH + CH)
        q = queries[rows, cols]
        v = jnp.concatenate([vals[k_rows, cols], ones], axis=1)
        outs = []
        for half in (left, jnp.logical_not(left)):
            s = lax.dot_general(
                jnp.where(half, q, BF16(0)),
                keys[k_rows, cols],
                (((1,), (1,)), ((), ())),
                preferred_element_type=F32,
            )
            s = s + hide[block]
            p = jnp.exp(s - jnp.max(s, axis=1, keepdims=True)).astype(BF16)
            o = jnp.dot(p, v, preferred_element_type=F32)
            outs.append(o[:, :CH] / o[:, CH:])
        mixed[rows, cols] = jnp.where(left, outs[0], outs[1]).astype(BF16)


def context_rows(src, target, count, head_w, keys, vals):
    rows = slice(target, target + count)
    keys[rows, :] = jnp.dot(src, head_w[:, D : 2 * D], preferred_element_type=F32).astype(BF16)
    vals[rows, :] = jnp.dot(src, head_w[:, 2 * D :], preferred_element_type=F32).astype(BF16)


def layer_kernel(
    raw_hbm,
    lens_ref,
    lens_smem,
    first_kernel,
    first_bias,
    second_kernel,
    second_bias,
    gain,
    embed_hbm,
    head_hbm,
    out_hbm,
    encoded,
    raw,
    low,
    high,
    kext,
    w1,
    w2,
    rows32,
    x_late,
    x_early,
    ycat,
    lower,
    second_out,
    embed_w,
    head_w,
    out_w,
    embedded,
    normed,
    before,
    after,
    queries,
    keys,
    vals,
    mixed,
    hide,
    load_sems,
    send_sems,
    recv_sems,
):
    inner = lax.axis_size("inner")
    devices = lax.axis_size("seq") * inner
    device = lax.axis_index("seq") * inner + lax.axis_index("inner")
    right_id = lax.rem(device + 1, devices)
    left_id = lax.rem(device + devices - 1, devices)
    right = (right_id // inner, lax.rem(right_id, inner))
    left = (left_id // inner, lax.rem(left_id, inner))
    barrier = pltpu.get_barrier_semaphore()
    for neighbour in (left, right):
        pl.semaphore_signal(barrier, inc=1, device_id=neighbour, device_id_type=MESH)

    def load(source, target, index):
        copy = pltpu.make_async_copy(source, target, load_sems.at[index])
        copy.start()
        return copy

    def send(source, target, index, neighbour):
        copy = pltpu.make_async_remote_copy(
            src_ref=source,
            dst_ref=target,
            send_sem=send_sems.at[index],
            recv_sem=recv_sems.at[index],
            device_id=neighbour,
            device_id_type=MESH,
        )
        copy.start()
        return copy

    load_raw = load(raw_hbm, raw, 0)
    pl.semaphore_wait(barrier, 2)
    cap = raw_hbm.shape[1]
    send_low = send(raw_hbm.at[:, cap - SIDE : cap], low, 0, right)
    send_high = send(raw_hbm.at[:, 0:SIDE], high, 1, left)
    load_embed = load(embed_hbm, embed_w, 1)
    load_head = load(head_hbm, head_w, 2)
    load_out = load(out_hbm, out_w, 3)
    base, starts = bounds(device, devices, lens_ref, lens_smem)
    build_taps(first_kernel, first_bias, kext)
    build_first(kext, w1)
    build_second(second_kernel, w2)
    build_hide(device, devices, base, starts, hide)
    spots = device * SHARD + lax.broadcasted_iota(jnp.int32, (SHARD, 1), 0)
    unused_seg, pos = locate(spots, base, starts)
    joined = pos > 0
    load_raw.wait()
    send_low.wait_recv()
    send_high.wait_recv()
    select_rows(device, base, starts, raw, low, high, rows32)
    build_inputs(CUT, SHARD - CUT, joined, rows32, x_late)
    build_inputs(0, CUT, joined, rows32, x_early)

    convolve(SHARD - CUT, x_late, w1, w2, second_bias, ycat, lower, second_out)
    load_embed.wait()
    embed_rows(CUT, SHARD - CUT, second_out, embed_w, embedded)
    norm_rows(CUT, SHARD - CUT, embedded, gain, normed)
    send_tail = send(normed.at[SHARD - SPAN : SHARD, :], before.at[CTX - SPAN : CTX, :], 2, right)
    send_body = send(normed.at[SHARD - CTX : SHARD - SPAN, :], before.at[0 : CTX - SPAN, :], 3, right)

    convolve(CUT, x_early, w1, w2, second_bias, ycat, lower, second_out)
    embed_rows(0, CUT, second_out, embed_w, embedded)
    norm_rows(0, CUT, embedded, gain, normed)
    send_head = send(normed.at[0:SPAN, :], after, 4, left)

    load_head.wait()
    queries[...] = (
        jnp.dot(normed[...], head_w[:, 0:D], preferred_element_type=F32).astype(BF16) * BF16(0.125)
    )
    context_rows(normed[...], CTX, SHARD, head_w, keys, vals)
    send_tail.wait_recv()
    send_head.wait_recv()
    context_rows(after[...], CTX + SHARD, SPAN, head_w, keys, vals)
    context_rows(before[CTX - SPAN : CTX, :], CTX - SPAN, SPAN, head_w, keys, vals)

    def block_step(step, carry):
        @pl.when(step == 2)
        def rest():
            send_body.wait_recv()
            context_rows(before[0 : CTX - SPAN, :], 0, CTX - SPAN, head_w, keys, vals)

        attend_block(3 - step, queries, keys, vals, hide, mixed)
        return carry

    lax.fori_loop(0, SHARD // QB, block_step, 0)
    load_out.wait()
    encoded[...] = (
        embedded[...].astype(F32) + jnp.dot(mixed[...], out_w[...], preferred_element_type=F32)
    ).astype(BF16)
    for copy in (send_low, send_high, send_tail, send_body, send_head):
        copy.wait_send()


def on_device(
    log_mel,
    lengths,
    first_kernel,
    first_bias,
    second_kernel,
    second_bias,
    embed_weight,
    norm_gain,
    head_weight,
    output_weight,
):
    vmem = pl.BlockSpec(memory_space=pltpu.VMEM)
    smem = pl.BlockSpec(memory_space=pltpu.SMEM)
    hbm = pl.BlockSpec(memory_space=pl.ANY)
    late = SHARD - CUT
    return pl.pallas_call(
        layer_kernel,
        out_shape=jax.ShapeDtypeStruct((SHARD, D), BF16),
        in_specs=[hbm, vmem, smem, vmem, vmem, vmem, vmem, vmem, hbm, hbm, hbm],
        out_specs=vmem,
        scratch_shapes=[
            pltpu.VMEM((4 * MEL, log_mel.shape[0]), BF16),
            pltpu.VMEM((4 * MEL, SIDE), BF16),
            pltpu.VMEM((4 * MEL, SIDE), BF16),
            pltpu.VMEM((32, 256), F32),
            pltpu.VMEM((256, BINS * 256), BF16),
            pltpu.VMEM((768, 256), BF16),
            pltpu.VMEM((WIDE, 4 * MEL), F32),
            pltpu.VMEM((3 * late, 256), BF16),
            pltpu.VMEM((3 * CUT, 256), BF16),
            pltpu.VMEM((2, late, 768), BF16),
            pltpu.VMEM((2, late, CH), F32),
            pltpu.VMEM((late, BINS * CH), BF16),
            pltpu.VMEM((BINS * CH, D), BF16),
            pltpu.VMEM((D, 3 * D), BF16),
            pltpu.VMEM((D, D), BF16),
            pltpu.VMEM((SHARD, D), BF16),
            pltpu.VMEM((SHARD, D), BF16),
            pltpu.VMEM((CTX, D), BF16),
            pltpu.VMEM((SPAN, D), BF16),
            pltpu.VMEM((SHARD, D), BF16),
            pltpu.VMEM((KEY_ROWS, D), BF16),
            pltpu.VMEM((KEY_ROWS, D), BF16),
            pltpu.VMEM((SHARD, D), BF16),
            pltpu.VMEM((SHARD // QB, QB, QK), F32),
            pltpu.SemaphoreType.DMA((4,)),
            pltpu.SemaphoreType.DMA((5,)),
            pltpu.SemaphoreType.DMA((5,)),
        ],
        compiler_params=pltpu.CompilerParams(
            vmem_limit_bytes=56 * 2**20, collective_id=0, has_side_effects=True
        ),
        name="layer",
    )(
        log_mel.T,
        lengths.T,
        lengths.T,
        first_kernel,
        first_bias.reshape(1, -1),
        second_kernel,
        second_bias.reshape(1, -1),
        norm_gain.reshape(1, -1),
        embed_weight,
        head_weight,
        output_weight,
    )


def solution(mesh):
    return jax.shard_map(
        on_device,
        mesh=mesh,
        in_specs=(P(AXES, None), P(), P(), P(), P(), P(), P(), P(), P(), P()),
        out_specs=P(AXES, None),
        check_vma=False,
    )
```

time: 92.5 us -> 46.4 us (0.50)
  the two profiles are of different devices: /device:TPU:96 before, /device:TPU:0 now
where the time goes in v1:
time: 46.4 us; the launch traced here: 46.2 us
  Pallas kernels  43.9 us (95%)
  local copies, waits for them, and re-layouts  2.26 us (5%)
    pallas_call x1, Pallas kernels, on_device(): pl.pallas_call(layer_kernel, out_shape=jax.ShapeDtypeStruct((SHARD, D), B...  43.9 us
    unnamed x1, local copies, waits for them, and re-layouts  2.26 us

profile of v1, /device:TPU:0, one launch (start us, length us, event | category | flops | bytes accessed | tf_op | source)
XLA Modules:
  0.0 46.2 jit_solution(10147689772195410651)
XLA Ops:
  0.0 43.9 %layer.1 = bf16[512,1024]{1,0:T(8,128)(2,1)} custom-call(bf16[320,896]{1,0:T(8,128)(2,1)} %bitcast.5, s32[4,128]{1,0:T(4,128)} %bitcast.6, s32[4,128]{1,0:T(4,128)} %bitcast.7, bf16[9,128]{1,0:T(8,128)(2,1)} %first_kernel.1, f32[1,128]{1,0:T(1,128)} %bitcast.9, bf16[1152,128]{1,0:T(8,128)(2,1)} %second_kernel.1, f32[1,128]{1,0:T(1,128)} %bitcast.10, ...), custom_call_target="tpu_custom_call" | custom-call | tf_op jit(solution)/shard_map/layer/pallas_call | solution.py:356
  43.9 2.3 %copy.12 = bf16[512,1024]{1,0:T(8,128)(2,1)} copy(bf16[512,1024]{1,0:T(8,128)(2,1)} %layer.1) | data formatting | bytes 2097152

commit v2 on v1

--- a/solution.py
+++ b/solution.py
@@ -15,7 +15,7 @@
 D = 1024
 BINS = 20
 CUT = 192
-WIDE = 640
+MIDDLE = 128
 SIDE = 256
 QB = 128
 QK = 512
@@ -100,50 +100,40 @@
         w2[256 * a + CH : 256 * a + 256, CH : 2 * CH] = second_kernel[base : base + CH, :]
 
 
-def select_rows(device, base, starts, raw, low, high, rows32):
-    spots = device * SHARD - 64 + lax.broadcasted_iota(jnp.int32, (1, WIDE), 1)
+def pick(device, base, starts, first, far, owner_index, near):
+    spots = device * SHARD + first + lax.broadcasted_iota(jnp.int32, (1, SIDE), 1)
     seg, unused_pos = locate(spots, base, starts)
     owner = lax.shift_right_arithmetic(seg, 2)
-    parts = [
-        jnp.where(owner[:, :SIDE] == 0, low[...].astype(F32), raw[:, 128:384].astype(F32)),
-        raw[:, 384:512].astype(F32),
-        jnp.where(owner[:, WIDE - SIDE :] == 2, high[...].astype(F32), raw[:, 512:768].astype(F32)),
-    ]
-    rows32[...] = jnp.concatenate(parts, axis=1).T
-
-
-def build_inputs(begin, count, joined, rows32, x):
+    return jnp.where(owner == owner_index, far[...].astype(F32), near.astype(F32))
+
+
+def build_inputs(offset, begin, count, joined, rows32, x):
     here = joined[begin : begin + count]
-    now = rows32[64 + begin : 64 + begin + count, :]
-    before = jnp.where(here, rows32[63 + begin : 63 + begin + count, :], 0.0)
+    now = rows32[offset : offset + count, :]
+    before = jnp.where(here, rows32[offset - 1 : offset + count - 1, :], 0.0)
     ones = jnp.ones((count, 16), F32)
     kept = jnp.where(here, ones, 0.0)
     x[0:count, :] = jnp.concatenate([before[:, MEL:], kept], axis=1).astype(BF16)
     x[count : 2 * count, :] = jnp.concatenate(
         [before[:, 3 * MEL :], now[:, : 2 * MEL], ones], axis=1
     ).astype(BF16)
-    x[2 * count :, :] = jnp.concatenate([now[:, MEL:], ones], axis=1).astype(BF16)
-
-
-def convolve(count, x, w1, w2, second_bias, ycat, lower, second_out):
+    x[2 * count : 3 * count, :] = jnp.concatenate([now[:, MEL:], ones], axis=1).astype(BF16)
+
+
+def convolve(begin, count, x, w1, w2, second_bias, ycat, second_out):
     bias = second_bias[...]
-    lower[0, 0:count, :] = jnp.zeros((count, CH), F32)
-
-    def body(step, carry):
-        for u in range(10):
-            slot = u % 2
-            f = step * 10 + u
-            block = w1[:, pl.ds(pl.multiple_of(f * 256, 256), 256)]
-            for a in range(3):
-                y = jnp.dot(x[a * count : (a + 1) * count, :], block, preferred_element_type=F32)
-                ycat[slot, 0:count, 256 * a : 256 * a + 256] = jnp.maximum(y, 0.0).astype(BF16)
-            r = jnp.dot(ycat[slot, 0:count, :], w2[...], preferred_element_type=F32)
-            out = jnp.maximum(r[:, :CH] + lower[slot, 0:count, :] + bias, 0.0).astype(BF16)
-            lower[1 - slot, 0:count, :] = r[:, CH:]
-            second_out[0:count, pl.ds(pl.multiple_of(f * CH, CH), CH)] = out
-        return carry
-
-    lax.fori_loop(0, BINS // 10, body, 0)
+    lower = None
+    for f in range(BINS):
+        slot = f % 2
+        y = jnp.dot(x[0 : 3 * count, :], w1[:, 256 * f : 256 * f + 256], preferred_element_type=F32)
+        for a in range(3):
+            ycat[slot, 0:count, 256 * a : 256 * a + 256] = jnp.maximum(
+                y[a * count : (a + 1) * count], 0.0
+            ).astype(BF16)
+        r = jnp.dot(ycat[slot, 0:count, :], w2[...], preferred_element_type=F32)
+        total = r[:, :CH] + bias if lower is None else r[:, :CH] + lower + bias
+        lower = r[:, CH:]
+        second_out[begin : begin + count, CH * f : CH * f + CH] = jnp.maximum(total, 0.0).astype(BF16)
 
 
 def embed_rows(begin, count, second_out, embed_w, embedded):
@@ -207,6 +197,19 @@
 
 def layer_kernel(
     raw_hbm,
+    lens_hbm,
+    taps_hbm,
+    first_bias_hbm,
+    second_hbm,
+    second_bias_hbm,
+    gain_hbm,
+    embed_hbm,
+    head_hbm,
+    out_hbm,
+    encoded,
+    raw,
+    low,
+    high,
     lens_ref,
     lens_smem,
     first_kernel,
@@ -214,21 +217,12 @@
     second_kernel,
     second_bias,
     gain,
-    embed_hbm,
-    head_hbm,
-    out_hbm,
-    encoded,
-    raw,
-    low,
-    high,
     kext,
     w1,
     w2,
     rows32,
-    x_late,
-    x_early,
+    x,
     ycat,
-    lower,
     second_out,
     embed_w,
     head_w,
@@ -249,21 +243,29 @@
     inner = lax.axis_size("inner")
     devices = lax.axis_size("seq") * inner
     device = lax.axis_index("seq") * inner + lax.axis_index("inner")
+    has_left = device > 0
+    has_right = device < devices - 1
     right_id = lax.rem(device + 1, devices)
     left_id = lax.rem(device + devices - 1, devices)
     right = (right_id // inner, lax.rem(right_id, inner))
     left = (left_id // inner, lax.rem(left_id, inner))
     barrier = pltpu.get_barrier_semaphore()
-    for neighbour in (left, right):
-        pl.semaphore_signal(barrier, inc=1, device_id=neighbour, device_id_type=MESH)
+
+    @pl.when(has_left)
+    def greet_left():
+        pl.semaphore_signal(barrier, inc=1, device_id=left, device_id_type=MESH)
+
+    @pl.when(has_right)
+    def greet_right():
+        pl.semaphore_signal(barrier, inc=1, device_id=right, device_id_type=MESH)
 
     def load(source, target, index):
         copy = pltpu.make_async_copy(source, target, load_sems.at[index])
         copy.start()
         return copy
 
-    def send(source, target, index, neighbour):
-        copy = pltpu.make_async_remote_copy(
+    def remote(source, target, index, neighbour):
+        return pltpu.make_async_remote_copy(
             src_ref=source,
             dst_ref=target,
             send_sem=send_sems.at[index],
@@ -271,17 +273,64 @@
             device_id=neighbour,
             device_id_type=MESH,
         )
-        copy.start()
-        return copy
-
-    load_raw = load(raw_hbm, raw, 0)
-    pl.semaphore_wait(barrier, 2)
+
+    small = [
+        load(source, target, index)
+        for index, (source, target) in enumerate(
+            (
+                (lens_hbm, lens_ref),
+                (lens_hbm, lens_smem),
+                (taps_hbm, first_kernel),
+                (first_bias_hbm, first_bias),
+                (second_hbm, second_kernel),
+                (second_bias_hbm, second_bias),
+                (gain_hbm, gain),
+            )
+        )
+    ]
+    load_raw = load(raw_hbm, raw, 7)
     cap = raw_hbm.shape[1]
-    send_low = send(raw_hbm.at[:, cap - SIDE : cap], low, 0, right)
-    send_high = send(raw_hbm.at[:, 0:SIDE], high, 1, left)
-    load_embed = load(embed_hbm, embed_w, 1)
-    load_head = load(head_hbm, head_w, 2)
-    load_out = load(out_hbm, out_w, 3)
+    send_low = remote(raw_hbm.at[:, cap - SIDE : cap], low, 0, right)
+    send_high = remote(raw_hbm.at[:, 0:SIDE], high, 1, left)
+    send_tail = remote(
+        normed.at[SHARD - SPAN : SHARD, :], before.at[CTX - SPAN : CTX, :], 2, right
+    )
+    send_body = remote(
+        normed.at[SHARD - CTX : SHARD - SPAN, :], before.at[0 : CTX - SPAN, :], 3, right
+    )
+    send_head = remote(normed.at[0:SPAN, :], after, 4, left)
+
+    @pl.when(jnp.logical_not(has_left))
+    def clear_left():
+        low[...] = jnp.zeros_like(low)
+        before[...] = jnp.zeros_like(before)
+
+    @pl.when(jnp.logical_not(has_right))
+    def clear_right():
+        high[...] = jnp.zeros_like(high)
+        after[...] = jnp.zeros_like(after)
+
+    @pl.when(has_left & has_right)
+    def meet_both():
+        pl.semaphore_wait(barrier, 2)
+
+    @pl.when(jnp.logical_not(has_left & has_right))
+    def meet_one():
+        pl.semaphore_wait(barrier, 1)
+
+    @pl.when(has_right)
+    def start_low():
+        send_low.start()
+
+    @pl.when(has_left)
+    def start_high():
+        send_high.start()
+
+    load_embed = load(embed_hbm, embed_w, 8)
+    load_head = load(head_hbm, head_w, 9)
+    load_out = load(out_hbm, out_w, 10)
+    for copy in small:
+        copy.wait()
     base, starts = bounds(device, devices, lens_ref, lens_smem)
     build_taps(first_kernel, first_bias, kext)
     build_first(kext, w1)
@@ -291,38 +340,65 @@
     unused_seg, pos = locate(spots, base, starts)
     joined = pos > 0
     load_raw.wait()
-    send_low.wait_recv()
-    send_high.wait_recv()
-    select_rows(device, base, starts, raw, low, high, rows32)
-    build_inputs(CUT, SHARD - CUT, joined, rows32, x_late)
-    build_inputs(0, CUT, joined, rows32, x_early)
-
-    convolve(SHARD - CUT, x_late, w1, w2, second_bias, ycat, lower, second_out)
+    rows32[0:256, :] = raw[:, 256:512].astype(F32).T
+    build_inputs(128, CUT, MIDDLE, joined, rows32, x)
+    convolve(0, MIDDLE, x, w1, w2, second_bias, ycat, second_out)
+
+    @pl.when(has_right)
+    def land_high():
+        send_high.wait_recv()
+
+    far = pick(device, base, starts, CTX, high, 2, raw[:, 512:768])
+    rows32[...] = jnp.concatenate([raw[:, 384:512].astype(F32), far], axis=1).T
+    build_inputs(128, CTX, CUT, joined, rows32, x)
+    convolve(MIDDLE, CUT, x, w1, w2, second_bias, ycat, second_out)
     load_embed.wait()
-    embed_rows(CUT, SHARD - CUT, second_out, embed_w, embedded)
-    norm_rows(CUT, SHARD - CUT, embedded, gain, normed)
-    send_tail = send(normed.at[SHARD - SPAN : SHARD, :], before.at[CTX - SPAN : CTX, :], 2, right)
-    send_body = send(normed.at[SHARD - CTX : SHARD - SPAN, :], before.at[0 : CTX - SPAN, :], 3, right)
-
-    convolve(CUT, x_early, w1, w2, second_bias, ycat, lower, second_out)
+    embed_rows(CUT, CTX, second_out, embed_w, embedded)
+    norm_rows(CUT, CTX, embedded, gain, normed)
+
+    @pl.when(has_right)
+    def start_context():
+        send_tail.start()
+        send_body.start()
+
+    @pl.when(has_left)
+    def land_low():
+        send_low.wait_recv()
+
+    rows32[0:256, :] = pick(device, base, starts, -64, low, 0, raw[:, 128:384]).T
+    build_inputs(64, 0, CUT, joined, rows32, x)
+    convolve(0, CUT, x, w1, w2, second_bias, ycat, second_out)
     embed_rows(0, CUT, second_out, embed_w, embedded)
     norm_rows(0, CUT, embedded, gain, normed)
-    send_head = send(normed.at[0:SPAN, :], after, 4, left)
+
+    @pl.when(has_left)
+    def start_after():
+        send_head.start()
 
     load_head.wait()
     queries[...] = (
         jnp.dot(normed[...], head_w[:, 0:D], preferred_element_type=F32).astype(BF16) * BF16(0.125)
     )
     context_rows(normed[...], CTX, SHARD, head_w, keys, vals)
-    send_tail.wait_recv()
-    send_head.wait_recv()
+
+    @pl.when(has_left)
+    def land_tail():
+        send_tail.wait_recv()
+
+    @pl.when(has_right)
+    def land_after():
+        send_head.wait_recv()
+
     context_rows(after[...], CTX + SHARD, SPAN, head_w, keys, vals)
     context_rows(before[CTX - SPAN : CTX, :], CTX - SPAN, SPAN, head_w, keys, vals)
 
     def block_step(step, carry):
+        @pl.when((step == 2) & has_left)
+        def land_body():
+            send_body.wait_recv()
+
         @pl.when(step == 2)
         def rest():
-            send_body.wait_recv()
             context_rows(before[0 : CTX - SPAN, :], 0, CTX - SPAN, head_w, keys, vals)
 
         attend_block(3 - step, queries, keys, vals, hide, mixed)
@@ -333,8 +409,17 @@
     encoded[...] = (
         embedded[...].astype(F32) + jnp.dot(mixed[...], out_w[...], preferred_element_type=F32)
     ).astype(BF16)
-    for copy in (send_low, send_high, send_tail, send_body, send_head):
-        copy.wait_send()
+
+    @pl.when(has_right)
+    def sent_right():
+        send_low.wait_send()
+        send_tail.wait_send()
+        send_body.wait_send()
+
+    @pl.when(has_left)
+    def sent_left():
+        send_high.wait_send()
+        send_head.wait_send()
 
 
 def on_device(
@@ -349,28 +434,30 @@
     head_weight,
     output_weight,
 ):
-    vmem = pl.BlockSpec(memory_space=pltpu.VMEM)
-    smem = pl.BlockSpec(memory_space=pltpu.SMEM)
     hbm = pl.BlockSpec(memory_space=pl.ANY)
-    late = SHARD - CUT
     return pl.pallas_call(
         layer_kernel,
         out_shape=jax.ShapeDtypeStruct((SHARD, D), BF16),
-        in_specs=[hbm, vmem, smem, vmem, vmem, vmem, vmem, vmem, hbm, hbm, hbm],
-        out_specs=vmem,
+        in_specs=[hbm] * 10,
+        out_specs=pl.BlockSpec(memory_space=pltpu.VMEM),
         scratch_shapes=[
             pltpu.VMEM((4 * MEL, log_mel.shape[0]), BF16),
             pltpu.VMEM((4 * MEL, SIDE), BF16),
             pltpu.VMEM((4 * MEL, SIDE), BF16),
+            pltpu.VMEM(lengths.shape[::-1], jnp.int32),
+            pltpu.SMEM(lengths.shape[::-1], jnp.int32),
+            pltpu.VMEM((9, CH), BF16),
+            pltpu.VMEM((1, CH), F32),
+            pltpu.VMEM((9 * CH, CH), BF16),
+            pltpu.VMEM((1, CH), F32),
+            pltpu.VMEM((1, D), F32),
             pltpu.VMEM((32, 256), F32),
             pltpu.VMEM((256, BINS * 256), BF16),
             pltpu.VMEM((768, 256), BF16),
-            pltpu.VMEM((WIDE, 4 * MEL), F32),
-            pltpu.VMEM((3 * late, 256), BF16),
+            pltpu.VMEM((2 * CUT, 4 * MEL), F32),
             pltpu.VMEM((3 * CUT, 256), BF16),
-            pltpu.VMEM((2, late, 768), BF16),
-            pltpu.VMEM((2, late, CH), F32),
-            pltpu.VMEM((late, BINS * CH), BF16),
+            pltpu.VMEM((2, CUT, 768), BF16),
+            pltpu.VMEM((CTX, BINS * CH), BF16),
             pltpu.VMEM((BINS * CH, D), BF16),
             pltpu.VMEM((D, 3 * D), BF16),
             pltpu.VMEM((D, D), BF16),
@@ -383,7 +470,7 @@
             pltpu.VMEM((KEY_ROWS, D), BF16),
             pltpu.VMEM((SHARD, D), BF16),
             pltpu.VMEM((SHARD // QB, QB, QK), F32),
-            pltpu.SemaphoreType.DMA((4,)),
+            pltpu.SemaphoreType.DMA((11,)),
             pltpu.SemaphoreType.DMA((5,)),
             pltpu.SemaphoreType.DMA((5,)),
         ],
@@ -394,7 +481,6 @@
     )(
         log_mel.T,
         lengths.T,
-        lengths.T,
         first_kernel,
         first_bias.reshape(1, -1),
         second_kernel,

time: 46.4 us -> 40.3 us (0.87)
  the two profiles are of different devices: /device:TPU:0 before, /device:TPU:63 now
where the time goes in v2:
time: 40.3 us; the launch traced here: 40.2 us
  Pallas kernels  37.9 us (94%)
  local copies, waits for them, and re-layouts  2.26 us (6%)
    pallas_call x1, Pallas kernels, on_device(): pl.pallas_call(layer_kernel, out_shape=jax.ShapeDtypeStruct((SHARD, D), B...  37.9 us
    unnamed x1, local copies, waits for them, and re-layouts  2.26 us

profile of v2, /device:TPU:63, one launch (start us, length us, event | category | flops | bytes accessed | tf_op | source)
XLA Modules:
  0.0 40.2 jit_solution(10830461699840615244)
XLA Ops:
  0.0 37.9 %layer.1 = bf16[512,1024]{1,0:T(8,128)(2,1)} custom-call(bf16[320,896]{1,0:T(8,128)(2,1)} %bitcast.5, s32[4,128]{1,0:T(4,128)} %bitcast.7, bf16[9,128]{1,0:T(8,128)(2,1)} %taps_hbm.1, f32[1,128]{1,0:T(1,128)} %bitcast.8, bf16[1152,128]{1,0:T(8,128)(2,1)} %second_hbm.1, f32[1,128]{1,0:T(1,128)} %bitcast.9, f32[1,1024]{1,0:T(1,128)} %bitcast.6, ...), custom_call_target="tpu_custom_call" | custom-call | tf_op jit(solution)/shard_map/layer/pallas_call | solution.py:438
  37.9 2.3 %copy.12 = bf16[512,1024]{1,0:T(8,128)(2,1)} copy(bf16[512,1024]{1,0:T(8,128)(2,1)} %layer.1) | data formatting | bytes 2097152

commit v3 on v2

--- a/solution.py
+++ b/solution.py
@@ -77,19 +77,15 @@
     row = lax.broadcasted_iota(jnp.int32, (256, 32), 0)
     col = lax.broadcasted_iota(jnp.int32, (256, 32), 1)
     tap = (row >= MEL).astype(jnp.int32) + (row >= 2 * MEL).astype(jnp.int32)
-    mel = row - MEL * tap
+    off = col - 5 * tap
+    inside = (off >= 0) & (off <= 4) & (row < 3 * MEL)
+    when = jnp.where(inside, row - MEL * tap + 1 - off, -1)
+    always = jnp.where((row >= 3 * MEL) & (row - 3 * MEL + 15 == col), 1.0, 0.0)
     wide = kext[...].astype(BF16)
-
-    def body(f, carry):
-        off = mel - 4 * f + 1
-        inside = (off >= 0) & (off <= 4) & (row < 3 * MEL)
-        want = jnp.where(inside, 5 * tap + off, jnp.where(row >= 3 * MEL, row - 3 * MEL + 15, -1))
-        select = jnp.where(col == want, 1.0, 0.0).astype(BF16)
+    for f in range(BINS):
+        select = jnp.where(when == 4 * f, 1.0, always).astype(BF16)
         block = jnp.dot(select, wide, preferred_element_type=F32)
-        w1[:, pl.ds(pl.multiple_of(f * 256, 256), 256)] = block.astype(BF16)
-        return carry
-
-    lax.fori_loop(0, BINS, body, 0, unroll=4)
+        w1[:, 256 * f : 256 * f + 256] = block.astype(BF16)
 
 
 def build_second(second_kernel, w2):
@@ -143,15 +139,13 @@
 
 
 def norm_rows(begin, count, embedded, gain, normed):
-    def step(r, carry):
-        rows = pl.ds(pl.multiple_of(begin + r * 64, 64), 64)
-        values = embedded[rows, :].astype(F32)
+    for r in range(begin, begin + count, 64):
+        values = embedded[r : r + 64, :].astype(F32)
         center = values - jnp.mean(values, axis=1, keepdims=True)
         spread = jnp.mean(center * center, axis=1, keepdims=True)
-        normed[rows, :] = (center * lax.rsqrt(spread + 1e-05) * gain[...]).astype(BF16)
-        return carry
-
-    lax.fori_loop(0, count // 64, step, 0)
+        normed[CTX + r : CTX + r + 64, :] = (
+            center * lax.rsqrt(spread + 1e-05) * gain[...]
+        ).astype(BF16)
 
 
 def build_hide(device, devices, base, starts, hide):
@@ -165,9 +159,16 @@
         hide[block] = jnp.where((gap >= 0) & (gap <= LEFT_SPANS), 0.0, -1e30)
 
 
-def attend_block(block, queries, keys, vals, hide, mixed):
-    rows = pl.ds(pl.multiple_of(block * QB, QB), QB)
-    k_rows = pl.ds(pl.multiple_of(block * QB, QB), QK)
+def project(block, piece, mixed, embedded, out_w, encoded):
+    rows = slice(block * QB, block * QB + QB)
+    cols = slice(piece * 256, piece * 256 + 256)
+    total = jnp.dot(mixed[rows, :], out_w[:, cols], preferred_element_type=F32)
+    encoded[rows, cols] = (embedded[rows, cols].astype(F32) + total).astype(BF16)
+
+
+def attend_block(block, done, queries, keys, vals, hide, mixed, embedded, out_w, encoded):
+    rows = slice(block * QB, block * QB + QB)
+    k_rows = slice(block * QB, block * QB + QK)
     left = lax.broadcasted_iota(jnp.int32, (QB, CH), 1) < 64
     ones = jnp.ones((QK, CH), BF16)
     for pair in range(D // CH):
@@ -187,12 +188,12 @@
             o = jnp.dot(p, v, preferred_element_type=F32)
             outs.append(o[:, :CH] / o[:, CH:])
         mixed[rows, cols] = jnp.where(left, outs[0], outs[1]).astype(BF16)
-
-
-def context_rows(src, target, count, head_w, keys, vals):
-    rows = slice(target, target + count)
-    keys[rows, :] = jnp.dot(src, head_w[:, D : 2 * D], preferred_element_type=F32).astype(BF16)
-    vals[rows, :] = jnp.dot(src, head_w[:, 2 * D :], preferred_element_type=F32).astype(BF16)
+        if done is not None and pair % 2 == 1:
+            project(done, pair // 2, mixed, embedded, out_w, encoded)
+
+
+def head_rows(src, column, head_w):
+    return jnp.dot(src, head_w[:, column : column + D], preferred_element_type=F32).astype(BF16)
 
 
 def layer_kernel(
@@ -229,8 +230,6 @@
     out_w,
     embedded,
     normed,
-    before,
-    after,
     queries,
     keys,
     vals,
@@ -293,52 +292,53 @@
     send_low = remote(raw_hbm.at[:, cap - SIDE : cap], low, 0, right)
     send_high = remote(raw_hbm.at[:, 0:SIDE], high, 1, left)
     send_tail = remote(
-        normed.at[SHARD - SPAN : SHARD, :], before.at[CTX - SPAN : CTX, :], 2, right
+        normed.at[CTX + SHARD - SPAN : CTX + SHARD, :], normed.at[CTX - SPAN : CTX, :], 2, right
     )
     send_body = remote(
-        normed.at[SHARD - CTX : SHARD - SPAN, :], before.at[0 : CTX - SPAN, :], 3, right
+        normed.at[SHARD : CTX + SHARD - SPAN, :], normed.at[0 : CTX - SPAN, :], 3, right
     )
-    send_head = remote(normed.at[0:SPAN, :], after, 4, left)
+    send_head = remote(normed.at[CTX : CTX + SPAN, :], normed.at[CTX + SHARD :, :], 4, left)
 
     @pl.when(jnp.logical_not(has_left))
     def clear_left():
         low[...] = jnp.zeros_like(low)
-        before[...] = jnp.zeros_like(before)
+        normed[0:CTX, :] = jnp.zeros((CTX, D), BF16)
 
     @pl.when(jnp.logical_not(has_right))
     def clear_right():
         high[...] = jnp.zeros_like(high)
-        after[...] = jnp.zeros_like(after)
-
-    @pl.when(has_left & has_right)
-    def meet_both():
-        pl.semaphore_wait(barrier, 2)
-
-    @pl.when(jnp.logical_not(has_left & has_right))
-    def meet_one():
-        pl.semaphore_wait(barrier, 1)
-
-    @pl.when(has_right)
-    def start_low():
-        send_low.start()
-
-    @pl.when(has_left)
-    def start_high():
-        send_high.start()
-
-    load_embed = load(embed_hbm, embed_w, 8)
-    load_head = load(head_hbm, head_w, 9)
-    load_out = load(out_hbm, out_w, 10)
+        normed[CTX + SHARD :, :] = jnp.zeros((SPAN, D), BF16)
+
     for copy in small:
         copy.wait()
     base, starts = bounds(device, devices, lens_ref, lens_smem)
     build_taps(first_kernel, first_bias, kext)
-    build_first(kext, w1)
     build_second(second_kernel, w2)
     build_hide(device, devices, base, starts, hide)
     spots = device * SHARD + lax.broadcasted_iota(jnp.int32, (SHARD, 1), 0)
     unused_seg, pos = locate(spots, base, starts)
     joined = pos > 0
+
+    @pl.when(has_left & has_right)
+    def meet_both():
+        pl.semaphore_wait(barrier, 2)
+
+    @pl.when(jnp.logical_not(has_left & has_right))
+    def meet_one():
+        pl.semaphore_wait(barrier, 1)
+
+    @pl.when(has_right)
+    def start_low():
+        send_low.start()
+
+    @pl.when(has_left)
+    def start_high():
+        send_high.start()
+
+    load_embed = load(embed_hbm, embed_w, 8)
+    load_head = load(head_hbm, head_w, 9)
+    load_out = load(out_hbm, out_w, 10)
+    build_first(kext, w1)
     load_raw.wait()
     rows32[0:256, :] = raw[:, 256:512].astype(F32).T
     build_inputs(128, CUT, MIDDLE, joined, rows32, x)
@@ -376,39 +376,39 @@
         send_head.start()
 
     load_head.wait()
-    queries[...] = (
-        jnp.dot(normed[...], head_w[:, 0:D], preferred_element_type=F32).astype(BF16) * BF16(0.125)
-    )
-    context_rows(normed[...], CTX, SHARD, head_w, keys, vals)
+    queries[...] = head_rows(normed[CTX : CTX + SHARD, :], 0, head_w) * BF16(0.125)
 
     @pl.when(has_left)
     def land_tail():
         send_tail.wait_recv()
+
+    for column, target in ((D, keys), (2 * D, vals)):
+        target[CTX - SPAN : CTX + SHARD, :] = head_rows(
+            normed[CTX - SPAN : CTX + SHARD, :], column, head_w
+        )
+    load_out.wait()
+    shared = (queries, keys, vals, hide, mixed, embedded, out_w, encoded)
+    attend_block(2, None, *shared)
+
+    @pl.when(has_left)
+    def land_body():
+        send_body.wait_recv()
 
     @pl.when(has_right)
     def land_after():
         send_head.wait_recv()
 
-    context_rows(after[...], CTX + SHARD, SPAN, head_w, keys, vals)
-    context_rows(before[CTX - SPAN : CTX, :], CTX - SPAN, SPAN, head_w, keys, vals)
-
-    def block_step(step, carry):
-        @pl.when((step == 2) & has_left)
-        def land_body():
-            send_body.wait_recv()
-
-        @pl.when(step == 2)
-        def rest():
-            context_rows(before[0 : CTX - SPAN, :], 0, CTX - SPAN, head_w, keys, vals)
-
-        attend_block(3 - step, queries, keys, vals, hide, mixed)
-        return carry
-
-    lax.fori_loop(0, SHARD // QB, block_step, 0)
-    load_out.wait()
-    encoded[...] = (
-        embedded[...].astype(F32) + jnp.dot(mixed[...], out_w[...], preferred_element_type=F32)
-    ).astype(BF16)
+    around = jnp.concatenate([normed[0 : CTX - SPAN, :], normed[CTX + SHARD :, :]], axis=0)
+    for column, target in ((D, keys), (2 * D, vals)):
+        result = head_rows(around, column, head_w)
+        target[0 : CTX - SPAN, :] = result[: CTX - SPAN]
+        target[CTX + SHARD :, :] = result[CTX - SPAN :]
+    done = 2
+    for block in (3, 1, 0):
+        attend_block(block, done, *shared)
+        done = block
+    for piece in range(D // 256):
+        project(done, piece, mixed, embedded, out_w, encoded)
 
     @pl.when(has_right)
     def sent_right():
@@ -434,7 +434,7 @@
     head_weight,
     output_weight,
 ):
-    hbm = pl.BlockSpec(memory_space=pl.ANY)
+    hbm = pl.BlockSpec(memory_space=pltpu.HBM)
     return pl.pallas_call(
         layer_kernel,
         out_shape=jax.ShapeDtypeStruct((SHARD, D), BF16),
@@ -462,9 +462,7 @@
             pltpu.VMEM((D, 3 * D), BF16),
             pltpu.VMEM((D, D), BF16),
             pltpu.VMEM((SHARD, D), BF16),
-            pltpu.VMEM((SHARD, D), BF16),
-            pltpu.VMEM((CTX, D), BF16),
-            pltpu.VMEM((SPAN, D), BF16),
+            pltpu.VMEM((KEY_ROWS, D), BF16),
             pltpu.VMEM((SHARD, D), BF16),
             pltpu.VMEM((KEY_ROWS, D), BF16),
             pltpu.VMEM((KEY_ROWS, D), BF16),
@@ -475,20 +473,25 @@
             pltpu.SemaphoreType.DMA((5,)),
         ],
         compiler_params=pltpu.CompilerParams(
-            vmem_limit_bytes=56 * 2**20, collective_id=0, has_side_effects=True
+            vmem_limit_bytes=48 * 2**20, collective_id=0, has_side_effects=True
         ),
         name="layer",
     )(
-        log_mel.T,
-        lengths.T,
-        first_kernel,
-        first_bias.reshape(1, -1),
-        second_kernel,
-        second_bias.reshape(1, -1),
-        norm_gain.reshape(1, -1),
-        embed_weight,
-        head_weight,
-        output_weight,
+        *(
+            pltpu.with_memory_space_constraint(value, pltpu.HBM)
+            for value in (
+                log_mel.T,
+                lengths.T,
+                first_kernel,
+                first_bias.reshape(1, -1),
+                second_kernel,
+                second_bias.reshape(1, -1),
+                norm_gain.reshape(1, -1),
+                embed_weight,
+                head_weight,
+                output_weight,
+            )
+        )
     )
 
 

time: 40.3 us -> 37.7 us (0.935)
  the two profiles are of different devices: /device:TPU:63 before, /device:TPU:96 now
where the time goes in v3:
time: 37.7 us; the launch traced here: 37.5 us
  Pallas kernels  36.6 us (97%)
  local copies, waits for them, and re-layouts  0.97 us (3%)
    pallas_call x1, Pallas kernels, on_device(): pl.pallas_call(layer_kernel, out_shape=jax.ShapeDtypeStruct((SHARD, D), B...  36.6 us
    unnamed x1, local copies, waits for them, and re-layouts  0.97 us

profile of v3, /device:TPU:96, one launch (start us, length us, event | category | flops | bytes accessed | tf_op | source)
XLA Modules:
  0.0 37.5 jit_solution(3692850524463534546)
XLA Ops:
  0.0 36.6 %layer.1 = bf16[512,1024]{1,0:T(8,128)(2,1)S(1)} custom-call(bf16[320,896]{1,0:T(8,128)(2,1)} %bitcast.5, s32[4,128]{1,0:T(4,128)} %bitcast.7, bf16[9,128]{1,0:T(8,128)(2,1)} %taps_hbm.1, f32[1,128]{1,0:T(1,128)} %bitcast.8, bf16[1152,128]{1,0:T(8,128)(2,1)} %second_hbm.1, f32[1,128]{1,0:T(1,128)} %bitcast.9, f32[1,1024]{1,0:T(1,128)} %bitcast.6, ...), custom_call_target="tpu_custom_call" | custom-call | tf_op jit(solution)/shard_map/layer/pallas_call | solution.py:438
  36.6 1.0 %copy.12 = bf16[512,1024]{1,0:T(8,128)(2,1)} copy(bf16[512,1024]{1,0:T(8,128)(2,1)S(1)} %layer.1) | data formatting | bytes 2097152

commit v4 on v3

--- a/solution.py
+++ b/solution.py
@@ -289,14 +289,15 @@
     ]
     load_raw = load(raw_hbm, raw, 7)
     cap = raw_hbm.shape[1]
-    send_low = remote(raw_hbm.at[:, cap - SIDE : cap], low, 0, right)
-    send_high = remote(raw_hbm.at[:, 0:SIDE], high, 1, left)
+    send_low = remote(raw.at[:, cap - SIDE : cap], low, 0, right)
+    send_high = remote(raw.at[:, 0:SIDE], high, 1, left)
     send_tail = remote(
         normed.at[CTX + SHARD - SPAN : CTX + SHARD, :], normed.at[CTX - SPAN : CTX, :], 2, right
     )
     send_body = remote(
-        normed.at[SHARD : CTX + SHARD - SPAN, :], normed.at[0 : CTX - SPAN, :], 3, right
+        normed.at[2 * CTX : CTX + SHARD - SPAN, :], normed.at[MIDDLE : CTX - SPAN, :], 3, right
     )
+    send_middle = remote(normed.at[SHARD : 2 * CTX, :], normed.at[0:MIDDLE, :], 5, right)
     send_head = remote(normed.at[CTX : CTX + SPAN, :], normed.at[CTX + SHARD :, :], 4, left)
 
     @pl.when(jnp.logical_not(has_left))
@@ -319,6 +320,8 @@
     unused_seg, pos = locate(spots, base, starts)
     joined = pos > 0
 
+    load_raw.wait()
+
     @pl.when(has_left & has_right)
     def meet_both():
         pl.semaphore_wait(barrier, 2)
@@ -339,11 +342,18 @@
     load_head = load(head_hbm, head_w, 9)
     load_out = load(out_hbm, out_w, 10)
     build_first(kext, w1)
-    load_raw.wait()
     rows32[0:256, :] = raw[:, 256:512].astype(F32).T
     build_inputs(128, CUT, MIDDLE, joined, rows32, x)
     convolve(0, MIDDLE, x, w1, w2, second_bias, ycat, second_out)
 
+    load_embed.wait()
+    embed_rows(CUT, MIDDLE, second_out, embed_w, embedded)
+    norm_rows(CUT, MIDDLE, embedded, gain, normed)
+
+    @pl.when(has_right)
+    def start_middle():
+        send_middle.start()
+
     @pl.when(has_right)
     def land_high():
         send_high.wait_recv()
@@ -351,10 +361,9 @@
     far = pick(device, base, starts, CTX, high, 2, raw[:, 512:768])
     rows32[...] = jnp.concatenate([raw[:, 384:512].astype(F32), far], axis=1).T
     build_inputs(128, CTX, CUT, joined, rows32, x)
-    convolve(MIDDLE, CUT, x, w1, w2, second_bias, ycat, second_out)
-    load_embed.wait()
-    embed_rows(CUT, CTX, second_out, embed_w, embedded)
-    norm_rows(CUT, CTX, embedded, gain, normed)
+    convolve(0, CUT, x, w1, w2, second_bias, ycat, second_out)
+    embed_rows(CTX, CUT, second_out, embed_w, embedded)
+    norm_rows(CTX, CUT, embedded, gain, normed)
 
     @pl.when(has_right)
     def start_context():
@@ -392,6 +401,7 @@
 
     @pl.when(has_left)
     def land_body():
+        send_middle.wait_recv()
         send_body.wait_recv()
 
     @pl.when(has_right)
@@ -414,6 +424,7 @@
     def sent_right():
         send_low.wait_send()
         send_tail.wait_send()
+        send_middle.wait_send()
         send_body.wait_send()
 
     @pl.when(has_left)
@@ -457,7 +468,7 @@
             pltpu.VMEM((2 * CUT, 4 * MEL), F32),
             pltpu.VMEM((3 * CUT, 256), BF16),
             pltpu.VMEM((2, CUT, 768), BF16),
-            pltpu.VMEM((CTX, BINS * CH), BF16),
+            pltpu.VMEM((CUT, BINS * CH), BF16),
             pltpu.VMEM((BINS * CH, D), BF16),
             pltpu.VMEM((D, 3 * D), BF16),
             pltpu.VMEM((D, D), BF16),
@@ -469,8 +480,8 @@
             pltpu.VMEM((SHARD, D), BF16),
             pltpu.VMEM((SHARD // QB, QB, QK), F32),
             pltpu.SemaphoreType.DMA((11,)),
-            pltpu.SemaphoreType.DMA((5,)),
-            pltpu.SemaphoreType.DMA((5,)),
+            pltpu.SemaphoreType.DMA((6,)),
+            pltpu.SemaphoreType.DMA((6,)),
         ],
         compiler_params=pltpu.CompilerParams(
             vmem_limit_bytes=48 * 2**20, collective_id=0, has_side_effects=True

time: 37.7 us -> 35.1 us (0.931)
  Pallas kernels: 36.6 us -> 34 us
    pallas_call x1, Pallas kernels: 36.6 us -> 34 us  [on_device(): pl.pallas_call(layer_kernel, out_shape=jax.ShapeDtypeStruct((SHARD, D), B...]
where the time goes in v4:
time: 35.1 us; the launch traced here: 35 us
  Pallas kernels  34 us (97%)
  local copies, waits for them, and re-layouts  0.97 us (3%)
    pallas_call x1, Pallas kernels, on_device(): pl.pallas_call(layer_kernel, out_shape=jax.ShapeDtypeStruct((SHARD, D), B...  34 us
    unnamed x1, local copies, waits for them, and re-layouts  0.97 us

profile of v4, /device:TPU:96, one launch (start us, length us, event | category | flops | bytes accessed | tf_op | source)
XLA Modules:
  0.0 35.0 jit_solution(1996268239610163951)
XLA Ops:
  0.0 34.0 %layer.1 = bf16[512,1024]{1,0:T(8,128)(2,1)S(1)} custom-call(bf16[320,896]{1,0:T(8,128)(2,1)} %bitcast.5, s32[4,128]{1,0:T(4,128)} %bitcast.7, bf16[9,128]{1,0:T(8,128)(2,1)} %taps_hbm.1, f32[1,128]{1,0:T(1,128)} %bitcast.8, bf16[1152,128]{1,0:T(8,128)(2,1)} %second_hbm.1, f32[1,128]{1,0:T(1,128)} %bitcast.9, f32[1,1024]{1,0:T(1,128)} %bitcast.6, ...), custom_call_target="tpu_custom_call" | custom-call | tf_op jit(solution)/shard_map/layer/pallas_call | solution.py:449
  34.0 1.0 %copy.12 = bf16[512,1024]{1,0:T(8,128)(2,1)} copy(bf16[512,1024]{1,0:T(8,128)(2,1)S(1)} %layer.1) | data formatting | bytes 2097152

commit v5 on v4

--- a/solution.py
+++ b/solution.py
@@ -148,13 +148,12 @@
         ).astype(BF16)
 
 
-def build_hide(device, devices, base, starts, hide):
+def build_hide(device, devices, base, starts, query_code, hide):
     spots = device * SHARD - CTX + lax.broadcasted_iota(jnp.int32, (1, KEY_ROWS), 1)
     key_code = codes(*locate(spots, base, starts))
     key_code = jnp.where((spots >= 0) & (spots < devices * SHARD), key_code, -1000)
     for block in range(SHARD // QB):
-        q_spots = device * SHARD + block * QB + lax.broadcasted_iota(jnp.int32, (QB, 1), 0)
-        q_code = codes(*locate(q_spots, base, starts))
+        q_code = query_code[block * QB : block * QB + QB]
         gap = q_code - key_code[:, block * QB : block * QB + QK]
         hide[block] = jnp.where((gap >= 0) & (gap <= LEFT_SPANS), 0.0, -1e30)
 
@@ -315,10 +314,10 @@
     base, starts = bounds(device, devices, lens_ref, lens_smem)
     build_taps(first_kernel, first_bias, kext)
     build_second(second_kernel, w2)
-    build_hide(device, devices, base, starts, hide)
     spots = device * SHARD + lax.broadcasted_iota(jnp.int32, (SHARD, 1), 0)
-    unused_seg, pos = locate(spots, base, starts)
+    seg, pos = locate(spots, base, starts)
     joined = pos > 0
+    build_hide(device, devices, base, starts, codes(seg, pos), hide)
 
     load_raw.wait()
 

time: 35.1 us -> 35.1 us (level)
  no operation moved by 1% of the time
where the time goes in v5:
time: 35.1 us; the launch traced here: 35 us
  Pallas kernels  34 us (97%)
  local copies, waits for them, and re-layouts  0.97 us (3%)
    pallas_call x1, Pallas kernels, on_device(): pl.pallas_call(layer_kernel, out_shape=jax.ShapeDtypeStruct((SHARD, D), B...  34 us
    unnamed x1, local copies, waits for them, and re-layouts  0.97 us

profile of v5, /device:TPU:96, one launch (start us, length us, event | category | flops | bytes accessed | tf_op | source)
XLA Modules:
  0.0 35.0 jit_solution(8421051572995025960)
XLA Ops:
  0.0 34.0 %layer.1 = bf16[512,1024]{1,0:T(8,128)(2,1)S(1)} custom-call(bf16[320,896]{1,0:T(8,128)(2,1)} %bitcast.5, s32[4,128]{1,0:T(4,128)} %bitcast.7, bf16[9,128]{1,0:T(8,128)(2,1)} %taps_hbm.1, f32[1,128]{1,0:T(1,128)} %bitcast.8, bf16[1152,128]{1,0:T(8,128)(2,1)} %second_hbm.1, f32[1,128]{1,0:T(1,128)} %bitcast.9, f32[1,1024]{1,0:T(1,128)} %bitcast.6, ...), custom_call_target="tpu_custom_call" | custom-call | tf_op jit(solution)/shard_map/layer/pallas_call | solution.py:448
  34.0 1.0 %copy.12 = bf16[512,1024]{1,0:T(8,128)(2,1)} copy(bf16[512,1024]{1,0:T(8,128)(2,1)S(1)} %layer.1) | data formatting | bytes 2097152
